TPU v7x, 32 devices: a whole 2x2x4 slice. The times are simulated.
32 devices in a mesh: depth: 4 (over z), tile: 8 (over y, x, core).
Axes of the slice: x: 2, y: 2, z: 4, core: 2. Of those that a mesh axis runs over, the one named last changes fastest.
Arguments:
- density: bfloat16 [32, 256, 1024], P('depth', None, 'tile'), may hold values from 0 to 1
- view_zoom: float32 [2], replicated, may hold values from 0.5 to 0.9
- view_shift: float32 [2], replicated, may hold values from 0 to 16
- tf_weights: float32 [2, 4, 8], replicated, may hold values from 0.25 to 2
- perm_order: int32 [2, 4], replicated, may hold values from 0 to 3, each once within a row
Outputs:
- image: float32 [2, 4, 256, 1024], P(None, None, 'depth', 'tile')
All inputs are finite; a program needn't handle non-finite values.
Results may differ from a plain program's by a relative error of at most 0.0028.
Values may be sent and summed in bfloat16 or wider, within the bound.
A program may use at most 64 MiB of HBM per device.

v0:
```python
import jax
import jax.numpy as jnp
from jax import lax
from jax.sharding import PartitionSpec as P

RADIUS = 8
OCCLUSION_GAIN = 1.5
EXTINCTION = 0.5


def with_halo(block, sides, width):
    for axis, dim in sides:
        count = lax.axis_size(axis)
        forward = [(i, i + 1) for i in range(count - 1)]
        backward = [(target, source) for source, target in forward]
        low = lax.ppermute(
            lax.slice_in_dim(block, block.shape[dim] - width, None, axis=dim), axis, forward
        )
        high = lax.ppermute(lax.slice_in_dim(block, 0, width, axis=dim), axis, backward)
        block = jnp.concatenate([low, block, high], axis=dim)
    return block


def blur_weights(radius):
    offsets = jnp.arange(-radius, radius + 1, dtype=jnp.float32)
    tap_weights = jnp.exp(-offsets * offsets / 72.0)
    return tap_weights / jnp.sum(tap_weights)


def occlusion_of(padded, radius, depth_cells, width_cells):
    tap_weights = blur_weights(radius)
    tap_count = 2 * radius + 1
    row_count = padded.shape[1]
    along_depth = tap_weights[0] * padded[0:depth_cells].astype(jnp.float32)
    for tap_index in range(1, tap_count):
        along_depth = along_depth + tap_weights[tap_index] * padded[
            tap_index : tap_index + depth_cells
        ].astype(jnp.float32)
    padded_rows = jnp.pad(along_depth, ((0, 0), (radius, radius), (0, 0)))
    along_rows = tap_weights[0] * padded_rows[:, 0:row_count]
    for tap_index in range(1, tap_count):
        along_rows = (
            along_rows + tap_weights[tap_index] * padded_rows[:, tap_index : tap_index + row_count]
        )
    along_width = tap_weights[0] * along_rows[:, :, 0:width_cells]
    for tap_index in range(1, tap_count):
        along_width = (
            along_width
            + tap_weights[tap_index] * along_rows[:, :, tap_index : tap_index + width_cells]
        )
    return jnp.exp(-OCCLUSION_GAIN * along_width).astype(jnp.bfloat16)


def resample_table(view_zoom, view_shift, row_count):
    pixel_pos = jnp.arange(row_count, dtype=jnp.float32)
    where_at = view_zoom[:, None] * pixel_pos[None, :] + view_shift[:, None]
    cell_pos = jnp.arange(row_count, dtype=jnp.float32)
    interp_table = jnp.maximum(0.0, 1.0 - jnp.abs(where_at[:, :, None] - cell_pos[None, None, :]))
    return interp_table.reshape(-1, row_count).astype(jnp.bfloat16)


def render_slab(slab_density, slab_shade, interp_table, tf_weights, depth_total):
    view_count = tf_weights.shape[0]
    basis_count = tf_weights.shape[2]
    row_count = slab_density.shape[1]
    width_cells = slab_density.shape[2]

    def one_slice(state_pair, cell_pair):
        colour, passing = state_pair
        density_rows, shade_rows = cell_pair
        stacked = jnp.concatenate([density_rows, shade_rows], axis=1)
        sampled = jnp.dot(interp_table, stacked, preferred_element_type=jnp.float32)
        sampled = sampled.reshape(view_count, row_count, 2 * width_cells)
        sampled_density = sampled[:, :, :width_cells]
        sampled_shade = sampled[:, :, width_cells:]
        values = jnp.zeros((view_count, 4, row_count, width_cells), jnp.float32)
        for basis_index in range(basis_count):
            offset = sampled_density * (basis_count - 1) - basis_index
            bump_value = jnp.exp(-0.5 * offset * offset)
            values = values + tf_weights[:, :, basis_index][:, :, None, None] * bump_value[:, None]
        opacity = 1.0 - jnp.exp(-(EXTINCTION / depth_total) * values[:, 3])
        lit_part = sampled_shade * opacity
        emitted = jnp.concatenate([values[:, 0:3] * lit_part[:, None], opacity[:, None]], axis=1)
        colour = colour + passing[:, None] * emitted
        passing = passing * (1.0 - opacity)
        return ((colour, passing), None)

    initial = (
        jnp.zeros((view_count, 4, row_count, width_cells), jnp.float32),
        jnp.ones((view_count, row_count, width_cells), jnp.float32),
    )
    final_state, _ = lax.scan(one_slice, initial, (slab_density, slab_shade))
    return final_state[0].astype(jnp.bfloat16)


def local(density, view_zoom, view_shift, tf_weights, perm_order):
    depth_cells = density.shape[0]
    row_count = density.shape[1]
    width_cells = density.shape[2]
    slab_count = lax.axis_size("depth")
    depth_total = depth_cells * slab_count
    padded = with_halo(density, (("depth", 0), ("tile", 2)), RADIUS)
    shade = occlusion_of(padded, RADIUS, depth_cells, width_cells)
    interp_table = resample_table(view_zoom, view_shift, row_count)
    slab_rgba = render_slab(density, shade, interp_table, tf_weights, depth_total)
    slot_ids = jnp.arange(slab_count, dtype=jnp.int32)
    selector = (perm_order[:, :, None] == slot_ids[None, None, :]).astype(jnp.bfloat16)
    ordered = jnp.einsum(
        "vqj,jvcrx->vqcrx",
        selector,
        lax.all_to_all(slab_rgba[None], "depth", split_axis=3, concat_axis=0, tiled=True),
        preferred_element_type=jnp.float32,
    )
    running = jnp.cumprod(1.0 - ordered[:, :, 3], axis=1)
    leading_ones = jnp.ones_like(running[:, 0:1])
    ahead_pass = jnp.concatenate([leading_ones, running[:, :-1]], axis=1)
    return jnp.sum(ahead_pass[:, :, None] * ordered, axis=1)


def solution(mesh):
    placed = (P("depth", None, "tile"), P(), P(), P(), P())
    return jax.shard_map(
        local, mesh=mesh, in_specs=placed, out_specs=P(None, None, "depth", "tile"), check_vma=False
    )
```

profile of v0, /device:TPU:4, one launch (start us, length us, event | category | flops | bytes accessed | tf_op | source)
XLA Modules:
  0.0 164.9 jit_solution(16466884867182730106)
XLA Ops:
  0.0 1.2 copy.51
  1.3 3.5 %collective-permute-start = (bf16[8,256,128]{1,2,0:T(8,128)(2,1)S(1)}, bf16[8,256,128]{1,2,0:T(8,128)(2,1)S(1)}, u32[]{:S(2)}, u32[]{:S(2)}) collective-permute-start(bf16[8,256,128]{1,2,0:T(8,128)(2,1)S(1)} %copy.51), channel_id=1, source_target_pairs={{0,8},{8,16},{16,24},{1,9},{9,17},{17,25},{2,10},{10,18},{18,26},{... | collective-permute-start | bytes 1572872 | tf_op jit(solution)/shard_map/ppermute | solution.py:16
  4.8 1.3 collective-permute-start.1
  6.1 0.8 copy.54
  6.9 0.7 add_bitcast_fusion
  8.9 7.0 %collective-permute-done = bf16[8,256,128]{1,2,0:T(8,128)(2,1)S(1)} collective-permute-done((bf16[8,256,128]{1,2,0:T(8,128)(2,1)S(1)}, bf16[8,256,128]{1,2,0:T(8,128)(2,1)S(1)}, u32[]{:S(2)}, u32[]{:S(2)}) %collective-permute-start) | collective-permute-done | bytes 524320 | tf_op jit(solution)/shard_map/ppermute | solution.py:16
  15.9 4.1 %collective-permute-done.1 = bf16[8,256,128]{1,2,0:T(8,128)(2,1)S(1)} collective-permute-done((bf16[8,256,128]{1,2,0:T(8,128)(2,1)S(1)}, bf16[8,256,128]{1,2,0:T(8,128)(2,1)S(1)}, u32[]{:S(2)}, u32[]{:S(2)}) %collective-permute-start.1) | collective-permute-done | bytes 524320 | tf_op jit(solution)/shard_map/ppermute | solution.py:19
  20.1 1.9 %collective-permute-start.2 = (bf16[24,256,8]{1,2,0:T(8,128)(2,1)S(1)}, bf16[24,256,8]{1,2,0:T(8,128)(2,1)S(1)}, u32[]{:S(2)}, u32[]{:S(2)}) collective-permute-start(bf16[24,256,8]{1,2,0:T(8,128)(2,1)S(1)} %get-tuple-element.190), channel_id=1, source_target_pairs={{0,1},{1,2},{2,3},{3,4},{4,5},{5,6},{6,7},{8,9},{9,10},{10,11},{11... | collective-permute-start | bytes 294920 | tf_op jit(solution)/shard_map/ppermute | solution.py:16
  22.0 4.5 %collective-permute-start.3 = (bf16[24,256,8]{1,2,0:T(8,128)(2,1)S(1)}, bf16[24,256,8]{1,2,0:T(8,128)(2,1)S(1)}, u32[]{:S(2)}, u32[]{:S(2)}) collective-permute-start(bf16[24,256,8]{1,2,0:T(8,128)(2,1)S(1)} %get-tuple-element.191), channel_id=1, source_target_pairs={{1,0},{2,1},{3,2},{4,3},{5,4},{6,5},{7,6},{9,8},{10,9},{11,10},{12... | collective-permute-start | bytes 294920 | tf_op jit(solution)/shard_map/ppermute | solution.py:19
  26.5 0.7 fusion.83
  27.3 1.5 collective-permute-done.3
  28.9 12.5 %multiply_add_fusion.1 = f32[8,256,144]{1,2,0:T(8,128)S(1)} fusion(bf16[24,256,144]{1,2,0:T(8,128)(2,1)S(1)} %pad_maximum_fusion, f32[]{:T(128)} %bitcast.18, f32[]{:T(128)} %bitcast.17, f32[]{:T(128)} %bitcast.16, f32[]{:T(128)} %bitcast.15, f32[]{:T(128)} %bitcast.14, f32[]{:T(128)} %bitcast.13, f32[]{:T(128)} %bitcast.12, f32[]{:T(128)} %bitcast.11, ...), kind=kLoop, calls=%fused_computation.98 | loop fusion | flops 14745600 | bytes 11206724 | tf_op jit(solution)/shard_map/add | solution.py:36
  41.4 15.6 %fusion.38 = f32[8,256,144]{1,2,0:T(8,128)S(1)} fusion(f32[8,256,144]{1,2,0:T(8,128)S(1)} %multiply_add_fusion.1, f32[]{:T(128)} %bitcast.18, f32[]{:T(128)} %bitcast.17, f32[]{:T(128)} %bitcast.16, f32[]{:T(128)} %bitcast.15, f32[]{:T(128)} %bitcast.14, f32[]{:T(128)} %bitcast.13, f32[]{:T(128)} %bitcast.12, f32[]{:T(128)} %bitcast.11, f32[]{:T(128)} %bitcast.10, ...), kind=kLoop, calls=%fused_computation.82 | loop fusion | flops 9732096 | bytes 2359364 | tf_op jit(solution)/shard_map/add | solution.py:43
  56.9 12.8 %fusion.57 = bf16[8,256,128]{1,2,0:T(8,128)(2,1)S(1)} fusion(f32[8,256,144]{1,2,0:T(8,128)S(1)} %fusion.38, f32[]{:T(128)} %bitcast.18, f32[]{:T(128)} %bitcast.17, f32[]{:T(128)} %bitcast.16, f32[]{:T(128)} %bitcast.15, f32[]{:T(128)} %bitcast.14, f32[]{:T(128)} %bitcast.13, f32[]{:T(128)} %bitcast.12, f32[]{:T(128)} %bitcast.11, f32[]{:T(128)} %bitcast.10, ...), kind=kLoop, calls=%fused_computation.103 | loop fusion | flops 9175040 | bytes 18350148 | tf_op jit(solution)/shard_map/convert_element_type | solution.py:51
  69.7 72.9 %while.15 = (s32[]{:T(128)}, f32[2,4,256,128]{3,2,0,1:T(8,128)S(1)}, f32[2,256,128]{2,1,0:T(8,128)}, f32[2,4,8]{1,0,2:T(2,128)S(1)}, bf16[8,256,128]{2,1,0:T(8,1...) while((s32[]{:T(128)}, ...), condition=%wide.region_2.3_spmd.clone, body=%wide.region_1.2_spmd.clone.sunk | while | flops 75300864 | bytes 19140008 | solution.py:92
  69.8 0.8 copy-done
  70.7 0.9 dynamic-slice_bitcast_fusion.2
  72.1 1.3 multiply_exponential_fusion.2
  74.1 1.9 %multiply_add_fusion.3 = f32[2,4,256,128]{3,2,0,1:T(8,128)S(1)} fusion(f32[2,256,128]{2,1,0:T(8,128)} %get-tuple-element.271, f32[2,4]{0,1:T(4,128)S(1)} %copy.83, f32[2,256,128]{2,1,0:T(8,128)} %get-tuple-element.273, f32[2,4]{0,1:T(4,128)S(1)} %copy.84, f32[2,256,128]{2,1,0:T(8,128)} %get-tuple-element.275, f32[2,4]{0,1:T(4,128)S(1)} %copy.85, ...), kind=kLoop, calls=%fused_computation.4.clone.1 | loop fusion | flops 3932160 | bytes 3145984 | tf_op jit(solution)/shard_map/while/body/eval_jaxpr/add | solution.py:80
  76.1 0.8 fusion.90
  77.4 0.6 copy-done.1
  78.0 0.8 copy-done
  78.9 0.9 dynamic-slice_bitcast_fusion.2
  80.4 1.3 multiply_exponential_fusion.2
  82.4 1.9 %multiply_add_fusion.3 = f32[2,4,256,128]{3,2,0,1:T(8,128)S(1)} fusion(f32[2,256,128]{2,1,0:T(8,128)} %get-tuple-element.271, f32[2,4]{0,1:T(4,128)S(1)} %copy.83, f32[2,256,128]{2,1,0:T(8,128)} %get-tuple-element.273, f32[2,4]{0,1:T(4,128)S(1)} %copy.84, f32[2,256,128]{2,1,0:T(8,128)} %get-tuple-element.275, f32[2,4]{0,1:T(4,128)S(1)} %copy.85, ...), kind=kLoop, calls=%fused_computation.4.clone.1 | loop fusion | flops 3932160 | bytes 3145984 | tf_op jit(solution)/shard_map/while/body/eval_jaxpr/add | solution.py:80
  84.4 1.7 %fusion.90 = (f32[2,256,128]{2,1,0:T(8,128)}, f32[2,256,128]{2,1,0:T(8,128)S(1)}, f32[2,256,128]{2,1,0:T(8,128)S(1)}) fusion(f32[2,4,256,128]{3,2,0,1:T(8,128)S(1)} %multiply_add_fusion.3, f32[2,256,128]{2,1,0:T(8,128)} %get-tuple-element.301, pred[]{:T(512)S(6)} %compare.5, f32[2,256,256]{2,1,0:T(8,128)S(1)} %bitcast.77), kind=kLoop, calls=%fused_computation.26.clone.1 | loop fusion | flops 393216 | bytes 1572865 | tf_op jit(solution)/shard_map/while/body/eval_jaxpr/mul | solution.py:85
  86.6 0.6 copy-done.1
  87.3 0.8 copy-done
  88.2 0.9 dynamic-slice_bitcast_fusion.2
  89.6 1.3 multiply_exponential_fusion.2
  91.7 1.9 %multiply_add_fusion.3 = f32[2,4,256,128]{3,2,0,1:T(8,128)S(1)} fusion(f32[2,256,128]{2,1,0:T(8,128)} %get-tuple-element.271, f32[2,4]{0,1:T(4,128)S(1)} %copy.83, f32[2,256,128]{2,1,0:T(8,128)} %get-tuple-element.273, f32[2,4]{0,1:T(4,128)S(1)} %copy.84, f32[2,256,128]{2,1,0:T(8,128)} %get-tuple-element.275, f32[2,4]{0,1:T(4,128)S(1)} %copy.85, ...), kind=kLoop, calls=%fused_computation.4.clone.1 | loop fusion | flops 3932160 | bytes 3145984 | tf_op jit(solution)/shard_map/while/body/eval_jaxpr/add | solution.py:80
  93.6 1.7 %fusion.90 = (f32[2,256,128]{2,1,0:T(8,128)}, f32[2,256,128]{2,1,0:T(8,128)S(1)}, f32[2,256,128]{2,1,0:T(8,128)S(1)}) fusion(f32[2,4,256,128]{3,2,0,1:T(8,128)S(1)} %multiply_add_fusion.3, f32[2,256,128]{2,1,0:T(8,128)} %get-tuple-element.301, pred[]{:T(512)S(6)} %compare.5, f32[2,256,256]{2,1,0:T(8,128)S(1)} %bitcast.77), kind=kLoop, calls=%fused_computation.26.clone.1 | loop fusion | flops 393216 | bytes 1572865 | tf_op jit(solution)/shard_map/while/body/eval_jaxpr/mul | solution.py:85
  96.5 0.8 copy-done
  97.4 0.9 dynamic-slice_bitcast_fusion.2
  98.8 1.3 multiply_exponential_fusion.2
  100.9 1.9 %multiply_add_fusion.3 = f32[2,4,256,128]{3,2,0,1:T(8,128)S(1)} fusion(f32[2,256,128]{2,1,0:T(8,128)} %get-tuple-element.271, f32[2,4]{0,1:T(4,128)S(1)} %copy.83, f32[2,256,128]{2,1,0:T(8,128)} %get-tuple-element.273, f32[2,4]{0,1:T(4,128)S(1)} %copy.84, f32[2,256,128]{2,1,0:T(8,128)} %get-tuple-element.275, f32[2,4]{0,1:T(4,128)S(1)} %copy.85, ...), kind=kLoop, calls=%fused_computation.4.clone.1 | loop fusion | flops 3932160 | bytes 3145984 | tf_op jit(solution)/shard_map/while/body/eval_jaxpr/add | solution.py:80
  102.8 1.7 %fusion.90 = (f32[2,256,128]{2,1,0:T(8,128)}, f32[2,256,128]{2,1,0:T(8,128)S(1)}, f32[2,256,128]{2,1,0:T(8,128)S(1)}) fusion(f32[2,4,256,128]{3,2,0,1:T(8,128)S(1)} %multiply_add_fusion.3, f32[2,256,128]{2,1,0:T(8,128)} %get-tuple-element.301, pred[]{:T(512)S(6)} %compare.5, f32[2,256,256]{2,1,0:T(8,128)S(1)} %bitcast.77), kind=kLoop, calls=%fused_computation.26.clone.1 | loop fusion | flops 393216 | bytes 1572865 | tf_op jit(solution)/shard_map/while/body/eval_jaxpr/mul | solution.py:85
  105.1 0.6 copy-done.1
  105.7 0.8 copy-done
  106.6 0.9 dynamic-slice_bitcast_fusion.2
  108.1 1.3 multiply_exponential_fusion.2
  110.1 1.9 %multiply_add_fusion.3 = f32[2,4,256,128]{3,2,0,1:T(8,128)S(1)} fusion(f32[2,256,128]{2,1,0:T(8,128)} %get-tuple-element.271, f32[2,4]{0,1:T(4,128)S(1)} %copy.83, f32[2,256,128]{2,1,0:T(8,128)} %get-tuple-element.273, f32[2,4]{0,1:T(4,128)S(1)} %copy.84, f32[2,256,128]{2,1,0:T(8,128)} %get-tuple-element.275, f32[2,4]{0,1:T(4,128)S(1)} %copy.85, ...), kind=kLoop, calls=%fused_computation.4.clone.1 | loop fusion | flops 3932160 | bytes 3145984 | tf_op jit(solution)/shard_map/while/body/eval_jaxpr/add | solution.py:80
  112.0 1.7 %fusion.90 = (f32[2,256,128]{2,1,0:T(8,128)}, f32[2,256,128]{2,1,0:T(8,128)S(1)}, f32[2,256,128]{2,1,0:T(8,128)S(1)}) fusion(f32[2,4,256,128]{3,2,0,1:T(8,128)S(1)} %multiply_add_fusion.3, f32[2,256,128]{2,1,0:T(8,128)} %get-tuple-element.301, pred[]{:T(512)S(6)} %compare.5, f32[2,256,256]{2,1,0:T(8,128)S(1)} %bitcast.77), kind=kLoop, calls=%fused_computation.26.clone.1 | loop fusion | flops 393216 | bytes 1572865 | tf_op jit(solution)/shard_map/while/body/eval_jaxpr/mul | solution.py:85
  114.3 0.6 copy-done.1
  114.9 0.8 copy-done
  115.9 0.9 dynamic-slice_bitcast_fusion.2
  117.3 1.3 multiply_exponential_fusion.2
  119.3 1.9 %multiply_add_fusion.3 = f32[2,4,256,128]{3,2,0,1:T(8,128)S(1)} fusion(f32[2,256,128]{2,1,0:T(8,128)} %get-tuple-element.271, f32[2,4]{0,1:T(4,128)S(1)} %copy.83, f32[2,256,128]{2,1,0:T(8,128)} %get-tuple-element.273, f32[2,4]{0,1:T(4,128)S(1)} %copy.84, f32[2,256,128]{2,1,0:T(8,128)} %get-tuple-element.275, f32[2,4]{0,1:T(4,128)S(1)} %copy.85, ...), kind=kLoop, calls=%fused_computation.4.clone.1 | loop fusion | flops 3932160 | bytes 3145984 | tf_op jit(solution)/shard_map/while/body/eval_jaxpr/add | solution.py:80
  121.3 1.7 %fusion.90 = (f32[2,256,128]{2,1,0:T(8,128)}, f32[2,256,128]{2,1,0:T(8,128)S(1)}, f32[2,256,128]{2,1,0:T(8,128)S(1)}) fusion(f32[2,4,256,128]{3,2,0,1:T(8,128)S(1)} %multiply_add_fusion.3, f32[2,256,128]{2,1,0:T(8,128)} %get-tuple-element.301, pred[]{:T(512)S(6)} %compare.5, f32[2,256,256]{2,1,0:T(8,128)S(1)} %bitcast.77), kind=kLoop, calls=%fused_computation.26.clone.1 | loop fusion | flops 393216 | bytes 1572865 | tf_op jit(solution)/shard_map/while/body/eval_jaxpr/mul | solution.py:85
  124.2 0.8 copy-done
  125.1 0.9 dynamic-slice_bitcast_fusion.2
  126.5 1.3 multiply_exponential_fusion.2
  128.6 1.9 %multiply_add_fusion.3 = f32[2,4,256,128]{3,2,0,1:T(8,128)S(1)} fusion(f32[2,256,128]{2,1,0:T(8,128)} %get-tuple-element.271, f32[2,4]{0,1:T(4,128)S(1)} %copy.83, f32[2,256,128]{2,1,0:T(8,128)} %get-tuple-element.273, f32[2,4]{0,1:T(4,128)S(1)} %copy.84, f32[2,256,128]{2,1,0:T(8,128)} %get-tuple-element.275, f32[2,4]{0,1:T(4,128)S(1)} %copy.85, ...), kind=kLoop, calls=%fused_computation.4.clone.1 | loop fusion | flops 3932160 | bytes 3145984 | tf_op jit(solution)/shard_map/while/body/eval_jaxpr/add | solution.py:80
  130.5 1.7 %fusion.90 = (f32[2,256,128]{2,1,0:T(8,128)}, f32[2,256,128]{2,1,0:T(8,128)S(1)}, f32[2,256,128]{2,1,0:T(8,128)S(1)}) fusion(f32[2,4,256,128]{3,2,0,1:T(8,128)S(1)} %multiply_add_fusion.3, f32[2,256,128]{2,1,0:T(8,128)} %get-tuple-element.301, pred[]{:T(512)S(6)} %compare.5, f32[2,256,256]{2,1,0:T(8,128)S(1)} %bitcast.77), kind=kLoop, calls=%fused_computation.26.clone.1 | loop fusion | flops 393216 | bytes 1572865 | tf_op jit(solution)/shard_map/while/body/eval_jaxpr/mul | solution.py:85
  132.8 0.6 copy-done.1
  133.4 0.8 copy-done
  134.3 0.9 dynamic-slice_bitcast_fusion.2
  135.7 1.3 multiply_exponential_fusion.2
  137.8 1.9 %multiply_add_fusion.3 = f32[2,4,256,128]{3,2,0,1:T(8,128)S(1)} fusion(f32[2,256,128]{2,1,0:T(8,128)} %get-tuple-element.271, f32[2,4]{0,1:T(4,128)S(1)} %copy.83, f32[2,256,128]{2,1,0:T(8,128)} %get-tuple-element.273, f32[2,4]{0,1:T(4,128)S(1)} %copy.84, f32[2,256,128]{2,1,0:T(8,128)} %get-tuple-element.275, f32[2,4]{0,1:T(4,128)S(1)} %copy.85, ...), kind=kLoop, calls=%fused_computation.4.clone.1 | loop fusion | flops 3932160 | bytes 3145984 | tf_op jit(solution)/shard_map/while/body/eval_jaxpr/add | solution.py:80
  139.7 1.7 %fusion.90 = (f32[2,256,128]{2,1,0:T(8,128)}, f32[2,256,128]{2,1,0:T(8,128)S(1)}, f32[2,256,128]{2,1,0:T(8,128)S(1)}) fusion(f32[2,4,256,128]{3,2,0,1:T(8,128)S(1)} %multiply_add_fusion.3, f32[2,256,128]{2,1,0:T(8,128)} %get-tuple-element.301, pred[]{:T(512)S(6)} %compare.5, f32[2,256,256]{2,1,0:T(8,128)S(1)} %bitcast.77), kind=kLoop, calls=%fused_computation.26.clone.1 | loop fusion | flops 393216 | bytes 1572865 | tf_op jit(solution)/shard_map/while/body/eval_jaxpr/mul | solution.py:85
  142.0 0.6 copy-done.1
  143.1 19.1 %all_to_all.18 = bf16[1,2,4,256,128]{4,2,1,0,3:T(4,128)(2,1)S(1)} all-to-all(bf16[1,2,4,256,128]{4,2,1,0,3:T(4,128)(2,1)S(1)} %bitcast.78), channel_id=1, replica_groups=mesh['depth'=4,'tile'=8] {'depth'}, dimensions={3} | all-to-all | bytes 1048576 | tf_op jit(solution)/shard_map/all_to_all | solution.py:111
  162.2 0.8 fusion.73
  163.5 1.4 multiply_reduce_fusion
  (161 shorter events, 18.9 us)
Async XLA Ops:
  1.3 14.7 %collective-permute-start = (bf16[8,256,128]{1,2,0:T(8,128)(2,1)S(1)}, bf16[8,256,128]{1,2,0:T(8,128)(2,1)S(1)}, u32[]{:S(2)}, u32[]{:S(2)}) collective-permute-start(bf16[8,256,128]{1,2,0:T(8,128)(2,1)S(1)} %copy.51), channel_id=1, source_target_pairs={{0,8},{8,16},{16,24},{1,9},{9,17},{17,25},{2,10},{10,18},{18,26},{... | collective-permute-start | bytes 1572872 | tf_op jit(solution)/shard_map/ppermute | solution.py:16
  4.8 15.3 %collective-permute-start.1 = (bf16[8,256,128]{1,2,0:T(8,128)(2,1)S(1)}, bf16[8,256,128]{1,2,0:T(8,128)(2,1)S(1)}, u32[]{:S(2)}, u32[]{:S(2)}) collective-permute-start(bf16[8,256,128]{1,2,0:T(8,128)(2,1)S(1)} %copy.51), channel_id=1, source_target_pairs={{8,0},{16,8},{24,16},{9,1},{17,9},{25,17},{10,2},{18,10},{26,18},{... | collective-permute-start | bytes 1572872 | tf_op jit(solution)/shard_map/ppermute | solution.py:19
  20.1 7.2 %collective-permute-start.2 = (bf16[24,256,8]{1,2,0:T(8,128)(2,1)S(1)}, bf16[24,256,8]{1,2,0:T(8,128)(2,1)S(1)}, u32[]{:S(2)}, u32[]{:S(2)}) collective-permute-start(bf16[24,256,8]{1,2,0:T(8,128)(2,1)S(1)} %get-tuple-element.190), channel_id=1, source_target_pairs={{0,1},{1,2},{2,3},{3,4},{4,5},{5,6},{6,7},{8,9},{9,10},{10,11},{11... | collective-permute-start | bytes 294920 | tf_op jit(solution)/shard_map/ppermute | solution.py:16
  22.0 6.7 %collective-permute-start.3 = (bf16[24,256,8]{1,2,0:T(8,128)(2,1)S(1)}, bf16[24,256,8]{1,2,0:T(8,128)(2,1)S(1)}, u32[]{:S(2)}, u32[]{:S(2)}) collective-permute-start(bf16[24,256,8]{1,2,0:T(8,128)(2,1)S(1)} %get-tuple-element.191), channel_id=1, source_target_pairs={{1,0},{2,1},{3,2},{4,3},{5,4},{6,5},{7,6},{9,8},{10,9},{11,10},{12... | collective-permute-start | bytes 294920 | tf_op jit(solution)/shard_map/ppermute | solution.py:19
  69.7 0.8 copy-start
  77.0 1.0 copy-start.1
  78.0 0.8 copy-start
  86.2 1.0 copy-start.1
  87.3 0.8 copy-start
  95.4 1.0 copy-start.1
  96.5 0.8 copy-start
  104.7 1.0 copy-start.1
  105.7 0.8 copy-start
  113.9 1.0 copy-start.1
  114.9 0.8 copy-start
  123.1 1.0 copy-start.1
  124.2 0.8 copy-start
  132.4 1.0 copy-start.1
  133.4 0.8 copy-start
  141.6 1.0 copy-start.1
  142.7 19.5 %copy-start.2 = (s32[2,4]{1,0:T(2,128)S(1)}, s32[2,4]{1,0:T(2,128)}, u32[]{:S(2)}) copy-start(s32[2,4]{1,0:T(2,128)} %param.11) | copy-start | bytes 100
where the time goes:
time: 167 us; the launch traced here: 165 us
  other arithmetic  87.5 us (52%)
  local copies, waits for them, and re-layouts  30 us (18%)
  blocking collectives  19.1 us (11%)
  waiting for transfers between devices  12.6 us (8%)
  starting transfers between devices  11.3 us (7%)
  matrix products  3.66 us (2%)
    all_to_all x1, blocking collectives, local(): lax.all_to_all(slab_rgba[None], 'depth', split_axis=3, concat_axis=0, til...  19.1 us
    add x1, other arithmetic, occlusion_of(): along_rows + tap_weights[tap_index] * padded_rows[:, tap_index:tap_index...  15.6 us
    add x8, other arithmetic, one_slice(): values + tf_weights[:, :, basis_index][:, :, None, None] * bump_value[:,...  15.3 us
    mul x8, other arithmetic, one_slice(): passing = passing * (1.0 - opacity)  13 us
    convert_element_type x1, other arithmetic, occlusion_of(): return jnp.exp(-OCCLUSION_GAIN * along_width).astype(jnp.bfloat16)  12.8 us
    add x1, other arithmetic, occlusion_of(): along_depth + tap_weights[tap_index] * padded[tap_index:tap_index + depth...  12.5 us
    while x32, local copies, waits for them, and re-layouts  11.6 us
    exp x8, other arithmetic, one_slice(): bump_value = jnp.exp(-0.5 * offset * offset)  10.5 us
  transfers between devices with their start and end apart: 4, of which 3 were waited for; matrix products, arithmetic and copies ran while one was open for 2% of the time, Pallas kernels for 0%

commit v1 on v0

--- a/solution.py
+++ b/solution.py
@@ -108,7 +108,12 @@
     ordered = jnp.einsum(
         "vqj,jvcrx->vqcrx",
         selector,
-        lax.all_to_all(slab_rgba[None], "depth", split_axis=3, concat_axis=0, tiled=True),
+        jnp.concatenate(
+            lax.all_to_all(
+                jnp.stack(jnp.split(slab_rgba[None], lax.axis_size("depth"), axis=3)), "depth", 0, 0
+            ),
+            axis=0,
+        ),
         preferred_element_type=jnp.float32,
     )
     running = jnp.cumprod(1.0 - ordered[:, :, 3], axis=1)

time: 167 us -> 162 us (0.970)
  local copies, waits for them, and re-layouts: 30 us -> 24.9 us
    while x32 -> x1, local copies, waits for them, and re-layouts: 11.6 us -> 0.08 us  [render_slab(): final_state, _ = lax.scan(one_slice, initial, (slab_density, slab_shade))]
    dynamic_slice x16, local copies, waits for them, and re-layouts: 0.93 us -> 7.67 us  [render_slab(): final_state, _ = lax.scan(one_slice, initial, (slab_density, slab_shade))]
where the time goes in v1:
time: 162 us; the launch traced here: 160 us
  other arithmetic  88 us (54%)
  local copies, waits for them, and re-layouts  24.9 us (15%)
  blocking collectives  19.1 us (12%)
  waiting for transfers between devices  12.6 us (8%)
  starting transfers between devices  11.3 us (7%)
  matrix products  3.43 us (2%)
    all_to_all x1, blocking collectives, local(): lax.all_to_all(jnp.stack(jnp.split(slab_rgba[None], lax.axis_size('depth'...  19.1 us
    add x1, other arithmetic, occlusion_of(): along_rows + tap_weights[tap_index] * padded_rows[:, tap_index:tap_index...  15.5 us
    add x8, other arithmetic, one_slice(): values + tf_weights[:, :, basis_index][:, :, None, None] * bump_value[:,...  15.3 us
    convert_element_type x1, other arithmetic, occlusion_of(): return jnp.exp(-OCCLUSION_GAIN * along_width).astype(jnp.bfloat16)  13.4 us
    mul x8, other arithmetic, one_slice(): passing = passing * (1.0 - opacity)  13 us
    add x1, other arithmetic, occlusion_of(): along_depth + tap_weights[tap_index] * padded[tap_index:tap_index + depth...  12.4 us
    exp x8, other arithmetic, one_slice(): bump_value = jnp.exp(-0.5 * offset * offset)  10.5 us
    dynamic_slice x16, local copies, waits for them, and re-layouts, render_slab(): final_state, _ = lax.scan(one_slice, initial, (slab_density, slab_shade))  7.67 us
  transfers between devices with their start and end apart: 4, of which 3 were waited for; matrix products, arithmetic and copies ran while one was open for 2% of the time, Pallas kernels for 0%

profile of v1, /device:TPU:4, one launch (start us, length us, event | category | flops | bytes accessed | tf_op | source)
XLA Modules:
  0.0 160.0 jit_solution(15390359243734307297)
XLA Ops:
  0.0 1.2 copy.96
  1.3 3.5 %collective-permute-start = (bf16[8,256,128]{1,2,0:T(8,128)(2,1)S(1)}, bf16[8,256,128]{1,2,0:T(8,128)(2,1)S(1)}, u32[]{:S(2)}, u32[]{:S(2)}) collective-permute-start(bf16[8,256,128]{1,2,0:T(8,128)(2,1)S(1)} %copy.96), channel_id=1, source_target_pairs={{0,8},{8,16},{16,24},{1,9},{9,17},{17,25},{2,10},{10,18},{18,26},{... | collective-permute-start | bytes 1572872 | tf_op jit(solution)/shard_map/ppermute | solution.py:16
  4.8 1.3 collective-permute-start.1
  6.1 0.8 copy.99
  6.9 0.7 add_bitcast_fusion
  7.6 0.6 fusion.83
  8.3 0.6 broadcast_divide_fusion
  8.9 7.0 %collective-permute-done = bf16[8,256,128]{1,2,0:T(8,128)(2,1)S(1)} collective-permute-done((bf16[8,256,128]{1,2,0:T(8,128)(2,1)S(1)}, bf16[8,256,128]{1,2,0:T(8,128)(2,1)S(1)}, u32[]{:S(2)}, u32[]{:S(2)}) %collective-permute-start) | collective-permute-done | bytes 524320 | tf_op jit(solution)/shard_map/ppermute | solution.py:16
  15.9 4.1 %collective-permute-done.1 = bf16[8,256,128]{1,2,0:T(8,128)(2,1)S(1)} collective-permute-done((bf16[8,256,128]{1,2,0:T(8,128)(2,1)S(1)}, bf16[8,256,128]{1,2,0:T(8,128)(2,1)S(1)}, u32[]{:S(2)}, u32[]{:S(2)}) %collective-permute-start.1) | collective-permute-done | bytes 524320 | tf_op jit(solution)/shard_map/ppermute | solution.py:19
  20.1 1.9 %collective-permute-start.2 = (bf16[24,256,8]{1,2,0:T(8,128)(2,1)S(1)}, bf16[24,256,8]{1,2,0:T(8,128)(2,1)S(1)}, u32[]{:S(2)}, u32[]{:S(2)}) collective-permute-start(bf16[24,256,8]{1,2,0:T(8,128)(2,1)S(1)} %get-tuple-element.211), channel_id=1, source_target_pairs={{0,1},{1,2},{2,3},{3,4},{4,5},{5,6},{6,7},{8,9},{9,10},{10,11},{11... | collective-permute-start | bytes 294920 | tf_op jit(solution)/shard_map/ppermute | solution.py:16
  22.0 4.5 %collective-permute-start.3 = (bf16[24,256,8]{1,2,0:T(8,128)(2,1)S(1)}, bf16[24,256,8]{1,2,0:T(8,128)(2,1)S(1)}, u32[]{:S(2)}, u32[]{:S(2)}) collective-permute-start(bf16[24,256,8]{1,2,0:T(8,128)(2,1)S(1)} %get-tuple-element.212), channel_id=1, source_target_pairs={{1,0},{2,1},{3,2},{4,3},{5,4},{6,5},{7,6},{9,8},{10,9},{11,10},{12... | collective-permute-start | bytes 294920 | tf_op jit(solution)/shard_map/ppermute | solution.py:19
  26.5 0.7 fusion.84
  27.3 1.5 collective-permute-done.3
  28.9 12.4 %multiply_add_fusion.1 = f32[8,256,144]{1,2,0:T(8,128)S(1)} fusion(bf16[24,256,144]{1,2,0:T(8,128)(2,1)S(1)} %pad_maximum_fusion, f32[]{:T(128)} %bitcast.18, f32[]{:T(128)} %bitcast.17, f32[]{:T(128)} %bitcast.16, f32[]{:T(128)} %bitcast.15, f32[]{:T(128)} %bitcast.14, f32[]{:T(128)} %bitcast.13, f32[]{:T(128)} %bitcast.12, f32[]{:T(128)} %bitcast.11, ...), kind=kLoop, calls=%fused_computation.98 | loop fusion | flops 14745600 | bytes 11206724 | tf_op jit(solution)/shard_map/add | solution.py:36
  41.3 15.5 %fusion.38 = f32[8,256,144]{1,2,0:T(8,128)S(1)} fusion(f32[8,256,144]{1,2,0:T(8,128)S(1)} %multiply_add_fusion.1, f32[]{:T(128)} %bitcast.18, f32[]{:T(128)} %bitcast.17, f32[]{:T(128)} %bitcast.16, f32[]{:T(128)} %bitcast.15, f32[]{:T(128)} %bitcast.14, f32[]{:T(128)} %bitcast.13, f32[]{:T(128)} %bitcast.12, f32[]{:T(128)} %bitcast.11, f32[]{:T(128)} %bitcast.10, ...), kind=kLoop, calls=%fused_computation.82 | loop fusion | flops 9732096 | bytes 2359364 | tf_op jit(solution)/shard_map/add | solution.py:43
  56.8 13.4 %fusion.57 = bf16[8,256,128]{1,2,0:T(8,128)(2,1)} fusion(f32[8,256,144]{1,2,0:T(8,128)S(1)} %fusion.38, f32[]{:T(128)} %bitcast.18, f32[]{:T(128)} %bitcast.17, f32[]{:T(128)} %bitcast.16, f32[]{:T(128)} %bitcast.15, f32[]{:T(128)} %bitcast.14, f32[]{:T(128)} %bitcast.13, f32[]{:T(128)} %bitcast.12, f32[]{:T(128)} %bitcast.11, f32[]{:T(128)} %bitcast.10, ...), kind=kLoop, calls=%fused_computation.103 | loop fusion | flops 9175040 | bytes 18350148 | tf_op jit(solution)/shard_map/convert_element_type | solution.py:51
  70.2 68.1 %while.15 = (s32[]{:T(128)}, f32[2,4,256,128]{3,2,0,1:T(8,128)S(1)}, f32[2,256,128]{2,1,0:T(8,128)}, f32[2,4,8]{1,0,2:T(2,128)S(1)}, bf16[8,256,128]{2,1,0:T(8,1...) while((s32[]{:T(128)}, ...), condition=%wide.region_2.3_spmd.clone, body=%wide.region_1.2_spmd.clone.sunk | while | flops 75300864 | bytes 14945648 | solution.py:92
  70.2 0.8 constant_dynamic-slice_fusion.2
  71.1 0.9 dynamic-slice_bitcast_fusion.2
  72.5 1.3 multiply_exponential_fusion.2
  74.6 1.9 %multiply_add_fusion.3 = f32[2,4,256,128]{3,2,0,1:T(8,128)S(1)} fusion(f32[2,256,128]{2,1,0:T(8,128)} %get-tuple-element.296, f32[2,4]{0,1:T(4,128)S(1)} %copy.126, f32[2,256,128]{2,1,0:T(8,128)} %get-tuple-element.298, f32[2,4]{0,1:T(4,128)S(1)} %copy.127, f32[2,256,128]{2,1,0:T(8,128)} %get-tuple-element.300, f32[2,4]{0,1:T(4,128)S(1)} %copy.128, ...), kind=kLoop, calls=%fused_computation.4.clone.1 | loop fusion | flops 3932160 | bytes 3145984 | tf_op jit(solution)/shard_map/while/body/eval_jaxpr/add | solution.py:80
  76.5 0.8 fusion.91
  77.8 0.8 constant_dynamic-slice_fusion.2
  78.8 0.9 dynamic-slice_bitcast_fusion.2
  80.2 1.3 multiply_exponential_fusion.2
  82.3 1.9 %multiply_add_fusion.3 = f32[2,4,256,128]{3,2,0,1:T(8,128)S(1)} fusion(f32[2,256,128]{2,1,0:T(8,128)} %get-tuple-element.296, f32[2,4]{0,1:T(4,128)S(1)} %copy.126, f32[2,256,128]{2,1,0:T(8,128)} %get-tuple-element.298, f32[2,4]{0,1:T(4,128)S(1)} %copy.127, f32[2,256,128]{2,1,0:T(8,128)} %get-tuple-element.300, f32[2,4]{0,1:T(4,128)S(1)} %copy.128, ...), kind=kLoop, calls=%fused_computation.4.clone.1 | loop fusion | flops 3932160 | bytes 3145984 | tf_op jit(solution)/shard_map/while/body/eval_jaxpr/add | solution.py:80
  84.2 1.7 %fusion.91 = (f32[2,256,128]{2,1,0:T(8,128)}, f32[2,256,128]{2,1,0:T(8,128)S(1)}, f32[2,256,128]{2,1,0:T(8,128)S(1)}) fusion(f32[2,4,256,128]{3,2,0,1:T(8,128)S(1)} %multiply_add_fusion.3, f32[2,256,128]{2,1,0:T(8,128)} %get-tuple-element.326, pred[]{:T(512)S(6)} %compare.5, f32[2,256,256]{2,1,0:T(8,128)S(1)} %bitcast.82), kind=kLoop, calls=%fused_computation.26.clone.1 | loop fusion | flops 393216 | bytes 1572865 | tf_op jit(solution)/shard_map/while/body/eval_jaxpr/mul | solution.py:85
  86.1 0.4 fusion.92
  86.5 0.8 constant_dynamic-slice_fusion.2
  87.4 0.9 dynamic-slice_bitcast_fusion.2
  88.8 1.3 multiply_exponential_fusion.2
  90.9 1.9 %multiply_add_fusion.3 = f32[2,4,256,128]{3,2,0,1:T(8,128)S(1)} fusion(f32[2,256,128]{2,1,0:T(8,128)} %get-tuple-element.296, f32[2,4]{0,1:T(4,128)S(1)} %copy.126, f32[2,256,128]{2,1,0:T(8,128)} %get-tuple-element.298, f32[2,4]{0,1:T(4,128)S(1)} %copy.127, f32[2,256,128]{2,1,0:T(8,128)} %get-tuple-element.300, f32[2,4]{0,1:T(4,128)S(1)} %copy.128, ...), kind=kLoop, calls=%fused_computation.4.clone.1 | loop fusion | flops 3932160 | bytes 3145984 | tf_op jit(solution)/shard_map/while/body/eval_jaxpr/add | solution.py:80
  92.8 1.7 %fusion.91 = (f32[2,256,128]{2,1,0:T(8,128)}, f32[2,256,128]{2,1,0:T(8,128)S(1)}, f32[2,256,128]{2,1,0:T(8,128)S(1)}) fusion(f32[2,4,256,128]{3,2,0,1:T(8,128)S(1)} %multiply_add_fusion.3, f32[2,256,128]{2,1,0:T(8,128)} %get-tuple-element.326, pred[]{:T(512)S(6)} %compare.5, f32[2,256,256]{2,1,0:T(8,128)S(1)} %bitcast.82), kind=kLoop, calls=%fused_computation.26.clone.1 | loop fusion | flops 393216 | bytes 1572865 | tf_op jit(solution)/shard_map/while/body/eval_jaxpr/mul | solution.py:85
  94.7 0.4 fusion.92
  95.1 0.8 constant_dynamic-slice_fusion.2
  96.1 0.9 dynamic-slice_bitcast_fusion.2
  97.5 1.3 multiply_exponential_fusion.2
  99.5 1.9 %multiply_add_fusion.3 = f32[2,4,256,128]{3,2,0,1:T(8,128)S(1)} fusion(f32[2,256,128]{2,1,0:T(8,128)} %get-tuple-element.296, f32[2,4]{0,1:T(4,128)S(1)} %copy.126, f32[2,256,128]{2,1,0:T(8,128)} %get-tuple-element.298, f32[2,4]{0,1:T(4,128)S(1)} %copy.127, f32[2,256,128]{2,1,0:T(8,128)} %get-tuple-element.300, f32[2,4]{0,1:T(4,128)S(1)} %copy.128, ...), kind=kLoop, calls=%fused_computation.4.clone.1 | loop fusion | flops 3932160 | bytes 3145984 | tf_op jit(solution)/shard_map/while/body/eval_jaxpr/add | solution.py:80
  101.5 1.7 %fusion.91 = (f32[2,256,128]{2,1,0:T(8,128)}, f32[2,256,128]{2,1,0:T(8,128)S(1)}, f32[2,256,128]{2,1,0:T(8,128)S(1)}) fusion(f32[2,4,256,128]{3,2,0,1:T(8,128)S(1)} %multiply_add_fusion.3, f32[2,256,128]{2,1,0:T(8,128)} %get-tuple-element.326, pred[]{:T(512)S(6)} %compare.5, f32[2,256,256]{2,1,0:T(8,128)S(1)} %bitcast.82), kind=kLoop, calls=%fused_computation.26.clone.1 | loop fusion | flops 393216 | bytes 1572865 | tf_op jit(solution)/shard_map/while/body/eval_jaxpr/mul | solution.py:85
  103.3 0.4 fusion.92
  103.7 0.8 constant_dynamic-slice_fusion.2
  104.7 0.9 dynamic-slice_bitcast_fusion.2
  106.1 1.3 multiply_exponential_fusion.2
  108.2 1.9 %multiply_add_fusion.3 = f32[2,4,256,128]{3,2,0,1:T(8,128)S(1)} fusion(f32[2,256,128]{2,1,0:T(8,128)} %get-tuple-element.296, f32[2,4]{0,1:T(4,128)S(1)} %copy.126, f32[2,256,128]{2,1,0:T(8,128)} %get-tuple-element.298, f32[2,4]{0,1:T(4,128)S(1)} %copy.127, f32[2,256,128]{2,1,0:T(8,128)} %get-tuple-element.300, f32[2,4]{0,1:T(4,128)S(1)} %copy.128, ...), kind=kLoop, calls=%fused_computation.4.clone.1 | loop fusion | flops 3932160 | bytes 3145984 | tf_op jit(solution)/shard_map/while/body/eval_jaxpr/add | solution.py:80
  110.1 1.7 %fusion.91 = (f32[2,256,128]{2,1,0:T(8,128)}, f32[2,256,128]{2,1,0:T(8,128)S(1)}, f32[2,256,128]{2,1,0:T(8,128)S(1)}) fusion(f32[2,4,256,128]{3,2,0,1:T(8,128)S(1)} %multiply_add_fusion.3, f32[2,256,128]{2,1,0:T(8,128)} %get-tuple-element.326, pred[]{:T(512)S(6)} %compare.5, f32[2,256,256]{2,1,0:T(8,128)S(1)} %bitcast.82), kind=kLoop, calls=%fused_computation.26.clone.1 | loop fusion | flops 393216 | bytes 1572865 | tf_op jit(solution)/shard_map/while/body/eval_jaxpr/mul | solution.py:85
  112.3 0.8 constant_dynamic-slice_fusion.2
  113.3 0.9 dynamic-slice_bitcast_fusion.2
  114.7 1.3 multiply_exponential_fusion.2
  116.8 1.9 %multiply_add_fusion.3 = f32[2,4,256,128]{3,2,0,1:T(8,128)S(1)} fusion(f32[2,256,128]{2,1,0:T(8,128)} %get-tuple-element.296, f32[2,4]{0,1:T(4,128)S(1)} %copy.126, f32[2,256,128]{2,1,0:T(8,128)} %get-tuple-element.298, f32[2,4]{0,1:T(4,128)S(1)} %copy.127, f32[2,256,128]{2,1,0:T(8,128)} %get-tuple-element.300, f32[2,4]{0,1:T(4,128)S(1)} %copy.128, ...), kind=kLoop, calls=%fused_computation.4.clone.1 | loop fusion | flops 3932160 | bytes 3145984 | tf_op jit(solution)/shard_map/while/body/eval_jaxpr/add | solution.py:80
  118.7 1.7 %fusion.91 = (f32[2,256,128]{2,1,0:T(8,128)}, f32[2,256,128]{2,1,0:T(8,128)S(1)}, f32[2,256,128]{2,1,0:T(8,128)S(1)}) fusion(f32[2,4,256,128]{3,2,0,1:T(8,128)S(1)} %multiply_add_fusion.3, f32[2,256,128]{2,1,0:T(8,128)} %get-tuple-element.326, pred[]{:T(512)S(6)} %compare.5, f32[2,256,256]{2,1,0:T(8,128)S(1)} %bitcast.82), kind=kLoop, calls=%fused_computation.26.clone.1 | loop fusion | flops 393216 | bytes 1572865 | tf_op jit(solution)/shard_map/while/body/eval_jaxpr/mul | solution.py:85
  121.0 0.8 constant_dynamic-slice_fusion.2
  121.9 0.9 dynamic-slice_bitcast_fusion.2
  123.4 1.3 multiply_exponential_fusion.2
  125.4 1.9 %multiply_add_fusion.3 = f32[2,4,256,128]{3,2,0,1:T(8,128)S(1)} fusion(f32[2,256,128]{2,1,0:T(8,128)} %get-tuple-element.296, f32[2,4]{0,1:T(4,128)S(1)} %copy.126, f32[2,256,128]{2,1,0:T(8,128)} %get-tuple-element.298, f32[2,4]{0,1:T(4,128)S(1)} %copy.127, f32[2,256,128]{2,1,0:T(8,128)} %get-tuple-element.300, f32[2,4]{0,1:T(4,128)S(1)} %copy.128, ...), kind=kLoop, calls=%fused_computation.4.clone.1 | loop fusion | flops 3932160 | bytes 3145984 | tf_op jit(solution)/shard_map/while/body/eval_jaxpr/add | solution.py:80
  127.3 1.7 %fusion.91 = (f32[2,256,128]{2,1,0:T(8,128)}, f32[2,256,128]{2,1,0:T(8,128)S(1)}, f32[2,256,128]{2,1,0:T(8,128)S(1)}) fusion(f32[2,4,256,128]{3,2,0,1:T(8,128)S(1)} %multiply_add_fusion.3, f32[2,256,128]{2,1,0:T(8,128)} %get-tuple-element.326, pred[]{:T(512)S(6)} %compare.5, f32[2,256,256]{2,1,0:T(8,128)S(1)} %bitcast.82), kind=kLoop, calls=%fused_computation.26.clone.1 | loop fusion | flops 393216 | bytes 1572865 | tf_op jit(solution)/shard_map/while/body/eval_jaxpr/mul | solution.py:85
  129.6 0.8 constant_dynamic-slice_fusion.2
  130.6 0.9 dynamic-slice_bitcast_fusion.2
  132.0 1.3 multiply_exponential_fusion.2
  134.0 1.9 %multiply_add_fusion.3 = f32[2,4,256,128]{3,2,0,1:T(8,128)S(1)} fusion(f32[2,256,128]{2,1,0:T(8,128)} %get-tuple-element.296, f32[2,4]{0,1:T(4,128)S(1)} %copy.126, f32[2,256,128]{2,1,0:T(8,128)} %get-tuple-element.298, f32[2,4]{0,1:T(4,128)S(1)} %copy.127, f32[2,256,128]{2,1,0:T(8,128)} %get-tuple-element.300, f32[2,4]{0,1:T(4,128)S(1)} %copy.128, ...), kind=kLoop, calls=%fused_computation.4.clone.1 | loop fusion | flops 3932160 | bytes 3145984 | tf_op jit(solution)/shard_map/while/body/eval_jaxpr/add | solution.py:80
  136.0 1.7 %fusion.91 = (f32[2,256,128]{2,1,0:T(8,128)}, f32[2,256,128]{2,1,0:T(8,128)S(1)}, f32[2,256,128]{2,1,0:T(8,128)S(1)}) fusion(f32[2,4,256,128]{3,2,0,1:T(8,128)S(1)} %multiply_add_fusion.3, f32[2,256,128]{2,1,0:T(8,128)} %get-tuple-element.326, pred[]{:T(512)S(6)} %compare.5, f32[2,256,256]{2,1,0:T(8,128)S(1)} %bitcast.82), kind=kLoop, calls=%fused_computation.26.clone.1 | loop fusion | flops 393216 | bytes 1572865 | tf_op jit(solution)/shard_map/while/body/eval_jaxpr/mul | solution.py:85
  138.4 19.1 %all_to_all.5 = bf16[4,1,2,4,64,128]{5,4,3,2,1,0:T(8,128)(2,1)S(1)} all-to-all(bf16[4,1,2,4,64,128]{5,4,3,2,1,0:T(8,128)(2,1)S(1)} %pad_maximum_fusion.1), channel_id=1, replica_groups=mesh['depth'=4,'tile'=8] {'depth'}, dimensions={0} | all-to-all | bytes 1048576 | tf_op jit(solution)/shard_map/all_to_all | solution.py:112
  157.5 0.5 fusion.74
  158.1 0.4 reduce_window.9
  158.6 1.4 multiply_reduce_fusion
  (130 shorter events, 14.5 us)
Async XLA Ops:
  1.3 14.7 %collective-permute-start = (bf16[8,256,128]{1,2,0:T(8,128)(2,1)S(1)}, bf16[8,256,128]{1,2,0:T(8,128)(2,1)S(1)}, u32[]{:S(2)}, u32[]{:S(2)}) collective-permute-start(bf16[8,256,128]{1,2,0:T(8,128)(2,1)S(1)} %copy.96), channel_id=1, source_target_pairs={{0,8},{8,16},{16,24},{1,9},{9,17},{17,25},{2,10},{10,18},{18,26},{... | collective-permute-start | bytes 1572872 | tf_op jit(solution)/shard_map/ppermute | solution.py:16
  4.8 15.3 %collective-permute-start.1 = (bf16[8,256,128]{1,2,0:T(8,128)(2,1)S(1)}, bf16[8,256,128]{1,2,0:T(8,128)(2,1)S(1)}, u32[]{:S(2)}, u32[]{:S(2)}) collective-permute-start(bf16[8,256,128]{1,2,0:T(8,128)(2,1)S(1)} %copy.96), channel_id=1, source_target_pairs={{8,0},{16,8},{24,16},{9,1},{17,9},{25,17},{10,2},{18,10},{26,18},{... | collective-permute-start | bytes 1572872 | tf_op jit(solution)/shard_map/ppermute | solution.py:19
  20.1 7.2 %collective-permute-start.2 = (bf16[24,256,8]{1,2,0:T(8,128)(2,1)S(1)}, bf16[24,256,8]{1,2,0:T(8,128)(2,1)S(1)}, u32[]{:S(2)}, u32[]{:S(2)}) collective-permute-start(bf16[24,256,8]{1,2,0:T(8,128)(2,1)S(1)} %get-tuple-element.211), channel_id=1, source_target_pairs={{0,1},{1,2},{2,3},{3,4},{4,5},{5,6},{6,7},{8,9},{9,10},{10,11},{11... | collective-permute-start | bytes 294920 | tf_op jit(solution)/shard_map/ppermute | solution.py:16
  22.0 6.7 %collective-permute-start.3 = (bf16[24,256,8]{1,2,0:T(8,128)(2,1)S(1)}, bf16[24,256,8]{1,2,0:T(8,128)(2,1)S(1)}, u32[]{:S(2)}, u32[]{:S(2)}) collective-permute-start(bf16[24,256,8]{1,2,0:T(8,128)(2,1)S(1)} %get-tuple-element.212), channel_id=1, source_target_pairs={{1,0},{2,1},{3,2},{4,3},{5,4},{6,5},{7,6},{9,8},{10,9},{11,10},{12... | collective-permute-start | bytes 294920 | tf_op jit(solution)/shard_map/ppermute | solution.py:19
  138.3 19.2 %copy-start = (s32[2,4]{1,0:T(2,128)S(1)}, s32[2,4]{1,0:T(2,128)}, u32[]{:S(2)}) copy-start(s32[2,4]{1,0:T(2,128)} %param.11) | copy-start | bytes 100
